TPU v7x, 256 devices: a whole 4x4x8 slice. The times are simulated.
256 devices in a mesh: seq: 32 (over z_hi, x, core), ch: 8 (over z_lo, y).
Axes of the slice: x: 4, y: 4, z: 8 (z_hi: 4, z_lo: 2; z = z_hi * 2 + z_lo), core: 2. Of those that a mesh axis runs over, the one named last changes fastest.
Arguments:
- query_act: bfloat16 [4096, 4096], P('seq', 'ch'), may hold values from -6 to 6
- key_act: bfloat16 [4096, 4096], P('seq', 'ch'), may hold values from -6 to 6
- value_act: bfloat16 [4096, 4096], P('seq', 'ch'), may hold values from -6 to 6
- filter_taps: bfloat16 [4096, 4096], P('seq', 'ch'), may hold values from -2 to 2
- out_grad: bfloat16 [4096, 4096], P('seq', 'ch'), may hold values from -6 to 6
- out_weight: bfloat16 [4096, 4096], P('ch'), may hold values from -0.09375 to 0.09375
Outputs:
- mixed_out: bfloat16 [4096, 4096], P('seq', 'ch')
- query_grad: bfloat16 [4096, 4096], P('seq', 'ch')
- key_grad: bfloat16 [4096, 4096], P('seq', 'ch')
- value_grad: bfloat16 [4096, 4096], P('seq', 'ch')
- filter_grad: float32 [4096, 4096], P('seq', 'ch')
All inputs are finite; a program needn't handle non-finite values.
Results may differ from a plain program's by a relative error of at most 0.02.
Values may be sent and summed in bfloat16 or wider, within the bound.
A program may use at most 128 MiB of HBM per device.

v0:
```python
import math
import jax
import jax.numpy as jnp
from jax import lax
from jax.sharding import PartitionSpec as P


def dft_tables(span_rows):
    period = 2 * span_rows
    frequency = jnp.arange(span_rows, dtype=jnp.int32)
    times_in = jnp.arange(span_rows, dtype=jnp.int32)
    times_out = jnp.arange(period, dtype=jnp.int32)
    parity_in = 1.0 - 2.0 * (times_in % 2).astype(jnp.float32)
    parity_out = 1.0 - 2.0 * (times_out % 2).astype(jnp.float32)
    phase_in = (frequency[:, None] * times_in[None, :] % period).astype(jnp.float32) * (
        2.0 * math.pi / period
    )
    cosine_rows = jnp.cos(phase_in)
    sine_rows = jnp.where(frequency[:, None] == 0, parity_in[None, :], -jnp.sin(phase_in))
    forward_t = jnp.concatenate([cosine_rows, sine_rows], axis=0)
    phase_out = (times_out[:, None] * frequency[None, :] % period).astype(jnp.float32) * (
        2.0 * math.pi / period
    )
    scaling = jnp.where(frequency == 0, 1.0, 2.0).astype(jnp.float32) / period
    cosinus_table_entries = jnp.cos(phase_out) * scaling[None, :]
    sine_cols = jnp.where(
        frequency[None, :] == 0,
        parity_out[:, None] / period,
        -jnp.sin(phase_out) * scaling[None, :],
    )
    inverse_t = jnp.concatenate([cosinus_table_entries, sine_cols], axis=1)
    alternate = 1.0 - 2.0 * (frequency % 2).astype(jnp.float32)
    top_sign = 1.0 - 2.0 * float(span_rows % 2)
    shift_sign = jnp.concatenate([alternate, jnp.where(frequency == 0, top_sign, alternate)])[
        :, None
    ]
    pair_mask = (frequency > 0).astype(jnp.float32)[:, None]
    return (forward_t, inverse_t, shift_sign, pair_mask)


def split_table(forward_t):
    table_high = forward_t.astype(jnp.bfloat16)
    kept_high = lax.optimization_barrier(table_high)
    table_low = (forward_t - kept_high.astype(jnp.float32)).astype(jnp.bfloat16)
    return (table_high, table_low)


def packed_product(first_spec, second_spec, pair_mask, conjugate):
    half_rows = first_spec.shape[-2] // 2
    first_real = first_spec[..., :half_rows, :]
    leading_quadrature_term = first_spec[..., half_rows:, :]
    second_real = second_spec[..., :half_rows, :]
    second_imag = second_spec[..., half_rows:, :]
    cross_real = leading_quadrature_term * second_imag
    if conjugate:
        real_part = first_real * second_real + pair_mask * cross_real
        imag_part = (
            pair_mask * (first_real * second_imag - leading_quadrature_term * second_real)
            + (1.0 - pair_mask) * cross_real
        )
    else:
        real_part = first_real * second_real - pair_mask * cross_real
        imag_part = (
            pair_mask * (first_real * second_imag + leading_quadrature_term * second_real)
            + (1.0 - pair_mask) * cross_real
        )
    return jnp.concatenate([real_part, imag_part], axis=-2)


def grouped_sums(spec_u, spec_h, spec_g, own_index, shift_sign, pair_mask):
    block_count = spec_u.shape[0]
    group_width = 8
    zero_spec = jnp.zeros(spec_u.shape[1:], jnp.float32)

    def fetch(spec, indices, usable):
        picked = spec[jnp.clip(indices, 0, block_count - 1)].astype(jnp.float32)
        return jnp.where(usable[:, None, None], picked, 0.0)

    def group_step(group, carry):
        conv_acc, ugrad_acc, hgrad_acc = carry
        indices = group * group_width + jnp.arange(group_width, dtype=jnp.int32)
        u_now = spec_u[indices].astype(jnp.float32)
        h_now = spec_h[indices].astype(jnp.float32)
        u_prev = fetch(spec_u, indices - 1, indices >= 1)
        lag = own_index - indices
        h_lag = fetch(spec_h, lag, lag >= 0)
        conv_acc = conv_acc + jnp.sum(
            packed_product(u_prev + shift_sign * u_now, h_lag, pair_mask, False), axis=0
        )
        lead = own_index + indices
        g_lead = fetch(spec_g, lead, lead <= block_count - 1)
        g_next = fetch(spec_g, lead + 1, lead + 1 <= block_count - 1)
        ahead = g_lead + shift_sign * g_next
        ugrad_acc = ugrad_acc + jnp.sum(packed_product(h_now, ahead, pair_mask, True), axis=0)
        hgrad_acc = hgrad_acc + jnp.sum(packed_product(u_now, ahead, pair_mask, True), axis=0)
        return (conv_acc, ugrad_acc, hgrad_acc)

    return lax.fori_loop(
        0, block_count // group_width, group_step, (zero_spec, zero_spec, zero_spec)
    )


def transform(blocks, table_high, table_low):
    high_part = jnp.einsum("pt,ntc->npc", table_high, blocks, preferred_element_type=jnp.float32)
    low_part = jnp.einsum("pt,ntc->npc", table_low, blocks, preferred_element_type=jnp.float32)
    return (high_part + low_part).astype(jnp.bfloat16)


def own_block(spec_u, spec_h, spec_g, own_index, inverse_t, shift_sign, pair_mask, span_rows):
    conv_spec, ugrad_spec, hgrad_spec = grouped_sums(
        spec_u, spec_h, spec_g, own_index, shift_sign, pair_mask
    )
    conv = jnp.dot(inverse_t[span_rows:], conv_spec, precision=lax.Precision.HIGHEST)
    u_grad = jnp.dot(inverse_t[:span_rows], ugrad_spec, precision=lax.Precision.HIGHEST)
    filter_grad = jnp.dot(inverse_t[:span_rows], hgrad_spec, precision=lax.Precision.HIGHEST)
    return (conv, u_grad, filter_grad)


def per_device(query_act, key_act, value_act, filter_taps, out_grad, out_weight):
    span_rows, feature_count = query_act.shape
    block_count = lax.axis_size("seq")
    own_index = lax.axis_index("seq")
    forward_t, inverse_t, shift_sign, pair_mask = dft_tables(span_rows)
    table_high, table_low = split_table(forward_t)
    product = (key_act.astype(jnp.float32) * value_act.astype(jnp.float32)).astype(jnp.bfloat16)
    gated_grad = lax.dot_general(
        lax.all_gather(out_grad, "ch", axis=1, tiled=True),
        out_weight,
        (((1,), (1,)), ((), ())),
        preferred_element_type=jnp.float32,
    )
    conv_grad = (gated_grad * query_act.astype(jnp.float32)).astype(jnp.bfloat16)
    own_u = transform(product[None], table_high, table_low)[0]
    own_h = transform(filter_taps[None], table_high, table_low)[0]
    own_g = transform(conv_grad[None], table_high, table_low)[0]
    received = (
        lax.all_gather(own_u, "seq", axis=0, tiled=True),
        lax.all_gather(own_h, "seq", axis=0, tiled=True),
        lax.all_gather(own_g, "seq", axis=0, tiled=True),
    )
    spec_u, spec_h, spec_g = [
        series.reshape(block_count, 2 * span_rows, feature_count) for series in received
    ]
    conv, u_grad, filter_grad = own_block(
        spec_u, spec_h, spec_g, own_index, inverse_t, shift_sign, pair_mask, span_rows
    )
    gated = (query_act.astype(jnp.float32) * conv).astype(jnp.bfloat16)
    partial_out = jnp.dot(gated, out_weight, preferred_element_type=jnp.float32)
    mixed_out = lax.psum_scatter(
        partial_out.astype(jnp.bfloat16), "ch", scatter_dimension=1, tiled=True
    )
    query_grad = (gated_grad * conv).astype(jnp.bfloat16)
    key_grad = (u_grad * value_act.astype(jnp.float32)).astype(jnp.bfloat16)
    value_grad = (u_grad * key_act.astype(jnp.float32)).astype(jnp.bfloat16)
    return (mixed_out, query_grad, key_grad, value_grad, filter_grad)


def solution(mesh):
    return jax.shard_map(
        per_device,
        mesh=mesh,
        in_specs=(
            P("seq", "ch"),
            P("seq", "ch"),
            P("seq", "ch"),
            P("seq", "ch"),
            P("seq", "ch"),
            P("ch", None),
        ),
        out_specs=(P("seq", "ch"), P("seq", "ch"), P("seq", "ch"), P("seq", "ch"), P("seq", "ch")),
        check_vma=False,
    )
```

profile of v0, /device:TPU:2, one launch (start us, length us, event | category | flops | bytes accessed | tf_op | source)
XLA Modules:
  0.0 563.4 jit_solution(4437507908320917075)
XLA Ops:
  11.6 42.8 %all-gather.9.cloned.1.call-done = bf16[128,4096]{1,0:T(8,128)(2,1)} async-done(((bf16[128,512]{1,0:T(8,128)(2,1)}), bf16[128,4096]{1,0:T(8,128)(2,1)}) %all-gather.9.cloned.1.call-update) | async-done | bytes 1048592 | tf_op jit(solution)/shard_map/all_gather | solution.py:127
  62.9 78.3 %all-gather.11.cloned.1.call-done = bf16[1,8192,512]{1,2,0:T(8,128)(2,1)} async-done(((bf16[1,256,512]{1,2,0:T(8,128)(2,1)}), bf16[1,8192,512]{1,2,0:T(8,128)(2,1)}) %all-gather.11.cloned.1.call-update) | async-done | bytes 8388624 | tf_op jit(solution)/shard_map/all_gather | solution.py:137
  141.2 11.6 %copy.13 = bf16[1,8192,512]{2,1,0:T(8,128)(2,1)} copy(bf16[1,8192,512]{1,2,0:T(8,128)(2,1)} %all-gather.11.cloned.1.call-done) | data formatting | bytes 16777216
  152.9 74.7 %all-gather.13.cloned.1.call-done = bf16[1,8192,512]{1,2,0:T(8,128)(2,1)} async-done(((bf16[1,256,512]{1,2,0:T(8,128)(2,1)}), bf16[1,8192,512]{1,2,0:T(8,128)(2,1)}) %all-gather.13.cloned.1.call-update) | async-done | bytes 8388624 | tf_op jit(solution)/shard_map/all_gather | solution.py:139
  227.5 12.0 %copy.14 = bf16[1,8192,512]{2,1,0:T(8,128)(2,1)} copy(bf16[1,8192,512]{1,2,0:T(8,128)(2,1)} %all-gather.13.cloned.1.call-done) | data formatting | bytes 16777216
  239.6 67.1 %all-gather.7.cloned.1.call-done = bf16[8192,512]{1,0:T(8,128)(2,1)} async-done(((bf16[256,512]{1,0:T(8,128)(2,1)}), bf16[8192,512]{1,0:T(8,128)(2,1)}) %all-gather.7.cloned.1.call-update) | async-done | bytes 8388624 | tf_op jit(solution)/shard_map/all_gather | solution.py:138
  306.7 203.5 %while.21 = (s32[]{:T(128)}, f32[256,512]{1,0:T(8,128)S(1)}, f32[256,512]{1,0:T(8,128)}, f32[256,512]{1,0:T(8,128)}, bf16[32,256,512]{2,1,0:T(8,128)(2,1)}, /*in...) while((s32[]{:T(128)}, f32[256,512]{1,0:T(8,128)S(1)}, ...), condition=%wide.region_4.5_spmd.clone.clone, body=%wide.region_0.4_spmd.clone.clone.sunk | while | flops 38148044 | bytes 155214800 | solution.py:98
  306.7 4.1 gather_fusion
  313.6 5.3 gather_fusion.1
  318.9 5.4 gather_fusion.2
  324.4 4.1 gather_fusion.3
  328.5 5.4 gather_fusion.4
  333.9 6.7 %multiply_add_fusion.9 = (f32[8,256,512]{2,1,0:T(8,128)}, f32[8,256,512]{2,1,0:T(8,128)S(1)}) fusion(bf16[8,256,512]{2,1,0:T(8,128)(2,1)} %gather_fusion.1, bf16[8,256,512]{2,1,0:T(8,128)(2,1)} %gather_fusion.2, f32[256]{0:T(256)S(1)} %get-tuple-element.514, pred[8]{0:T(512)(128)(4,1)S(1)} %add_compare_fusion.2, pred[8]{0:T(512)(128)(4,1)S(1)} %fusion.88, ...), kind=kLoop, calls=%fused_computation.11.clone.1 | loop fusion | flops 11534336 | bytes 16778264 | tf_op jit(solution)/shard_map/while/body/eval_jaxpr/add | solution.py:93
  342.4 5.4 gather_fusion.5
  364.4 5.3 gather_fusion.1
  369.8 5.4 gather_fusion.2
  375.2 4.1 gather_fusion.3
  379.3 5.4 gather_fusion.4
  384.7 6.7 %multiply_add_fusion.9 = (f32[8,256,512]{2,1,0:T(8,128)}, f32[8,256,512]{2,1,0:T(8,128)S(1)}) fusion(bf16[8,256,512]{2,1,0:T(8,128)(2,1)} %gather_fusion.1, bf16[8,256,512]{2,1,0:T(8,128)(2,1)} %gather_fusion.2, f32[256]{0:T(256)S(1)} %get-tuple-element.514, pred[8]{0:T(512)(128)(4,1)S(1)} %add_compare_fusion.2, pred[8]{0:T(512)(128)(4,1)S(1)} %fusion.88, ...), kind=kLoop, calls=%fused_computation.11.clone.1 | loop fusion | flops 11534336 | bytes 16778264 | tf_op jit(solution)/shard_map/while/body/eval_jaxpr/add | solution.py:93
  393.3 5.4 gather_fusion.5
  415.3 5.3 gather_fusion.1
  420.6 5.4 gather_fusion.2
  426.1 4.1 gather_fusion.3
  430.2 5.4 gather_fusion.4
  435.6 6.7 %multiply_add_fusion.9 = (f32[8,256,512]{2,1,0:T(8,128)}, f32[8,256,512]{2,1,0:T(8,128)S(1)}) fusion(bf16[8,256,512]{2,1,0:T(8,128)(2,1)} %gather_fusion.1, bf16[8,256,512]{2,1,0:T(8,128)(2,1)} %gather_fusion.2, f32[256]{0:T(256)S(1)} %get-tuple-element.514, pred[8]{0:T(512)(128)(4,1)S(1)} %add_compare_fusion.2, pred[8]{0:T(512)(128)(4,1)S(1)} %fusion.88, ...), kind=kLoop, calls=%fused_computation.11.clone.1 | loop fusion | flops 11534336 | bytes 16778264 | tf_op jit(solution)/shard_map/while/body/eval_jaxpr/add | solution.py:93
  444.1 5.4 gather_fusion.5
  466.1 5.3 gather_fusion.1
  471.5 5.4 gather_fusion.2
  481.0 5.4 gather_fusion.4
  486.4 6.7 %multiply_add_fusion.9 = (f32[8,256,512]{2,1,0:T(8,128)}, f32[8,256,512]{2,1,0:T(8,128)S(1)}) fusion(bf16[8,256,512]{2,1,0:T(8,128)(2,1)} %gather_fusion.1, bf16[8,256,512]{2,1,0:T(8,128)(2,1)} %gather_fusion.2, f32[256]{0:T(256)S(1)} %get-tuple-element.514, pred[8]{0:T(512)(128)(4,1)S(1)} %add_compare_fusion.2, pred[8]{0:T(512)(128)(4,1)S(1)} %fusion.88, ...), kind=kLoop, calls=%fused_computation.11.clone.1 | loop fusion | flops 11534336 | bytes 16778264 | tf_op jit(solution)/shard_map/while/body/eval_jaxpr/add | solution.py:93
  495.0 5.4 gather_fusion.5
  518.5 38.4 %reduce-scatter.2.cloned.1.call-done = bf16[128,512]{1,0:T(8,128)(2,1)} async-done(((bf16[128,4096]{1,0:T(8,128)(2,1)}), bf16[128,512]{1,0:T(8,128)(2,1)}) %reduce-scatter.2.cloned.1.call-update) | async-done | bytes 131088 | tf_op jit(solution)/shard_map/reduce_scatter | solution.py:149
  (214 shorter events, 94.5 us)
Async XLA Ops:
  7.2 53.0 %copy-start = (bf16[128,512]{1,0:T(8,128)(2,1)S(1)}, bf16[128,512]{1,0:T(8,128)(2,1)}, u32[]{:S(2)}) copy-start(bf16[128,512]{1,0:T(8,128)(2,1)} %param.11) | copy-start | bytes 393220
  7.2 47.2 %all-gather.9.cloned.1.call-start = ((), (), s32[]{:S(2)}) async-start(), calls=%async_computation.2 | async-start | bytes 1179648 | tf_op jit(solution)/shard_map/all_gather | solution.py:127
  7.9 133.3 %all-gather.11.cloned.1.call-start = ((), (), s32[]{:S(2)}) async-start(), calls=%async_computation.4 | async-start | bytes 8650752 | tf_op jit(solution)/shard_map/all_gather | solution.py:137
  11.5 46.9 %copy-start.15 = (bf16[128,512]{1,0:T(8,128)(2,1)S(1)}, bf16[128,512]{1,0:T(8,128)(2,1)}, u32[]{:S(2)}) copy-start(bf16[128,512]{1,0:T(8,128)(2,1)} %param.8) | copy-start | bytes 393220
  11.5 216.0 %all-gather.13.cloned.1.call-start = ((), (), s32[]{:S(2)}) async-start(), calls=%async_computation.5 | async-start | bytes 8650752 | tf_op jit(solution)/shard_map/all_gather | solution.py:139
  60.1 246.6 %all-gather.7.cloned.1.call-start = ((), (), s32[]{:S(2)}) async-start(), calls=%async_computation.1 | async-start | bytes 8650752 | tf_op jit(solution)/shard_map/all_gather | solution.py:138
  61.3 495.6 %reduce-scatter.2.cloned.1.call-start = ((), (), s32[]{:S(2)}) async-start(), calls=%async_computation.3 | async-start | bytes 1179648 | tf_op jit(solution)/shard_map/reduce_scatter | solution.py:149
  306.7 203.5 %copy-start.11 = (f32[128,512]{1,0:T(8,128)S(1)}, f32[128,512]{1,0:T(8,128)}, u32[]{:S(2)}) copy-start(f32[128,512]{1,0:T(8,128)} %copy-done.10) | copy-start | bytes 786436
  306.7 203.5 %copy-start.12 = (f32[256,128]{1,0:T(8,128)S(1)}, f32[256,128]{1,0:T(8,128)}, u32[]{:S(2)}) copy-start(f32[256,128]{1,0:T(8,128)} %get-tuple-element.404) | copy-start | bytes 393220
  333.8 6.7 %copy-start.2 = (f32[8,256,512]{2,1,0:T(8,128)S(1)}, f32[8,256,512]{2,1,0:T(8,128)}, u32[]{:S(2)}) copy-start(f32[8,256,512]{2,1,0:T(8,128)} %convert_select_fusion.2) | copy-start | bytes 12582916 | tf_op jit(solution)/shard_map/while
  350.1 2.2 copy-start.3
  355.1 1.0 copy-start.4
  355.1 1.2 copy-start.7
  384.7 6.7 %copy-start.2 = (f32[8,256,512]{2,1,0:T(8,128)S(1)}, f32[8,256,512]{2,1,0:T(8,128)}, u32[]{:S(2)}) copy-start(f32[8,256,512]{2,1,0:T(8,128)} %convert_select_fusion.2) | copy-start | bytes 12582916 | tf_op jit(solution)/shard_map/while
  400.9 2.2 copy-start.3
  405.9 1.0 copy-start.4
  405.9 1.2 copy-start.7
  435.6 6.7 %copy-start.2 = (f32[8,256,512]{2,1,0:T(8,128)S(1)}, f32[8,256,512]{2,1,0:T(8,128)}, u32[]{:S(2)}) copy-start(f32[8,256,512]{2,1,0:T(8,128)} %convert_select_fusion.2) | copy-start | bytes 12582916 | tf_op jit(solution)/shard_map/while
  451.8 2.2 copy-start.3
  456.8 1.0 copy-start.4
  456.8 1.2 copy-start.7
  486.4 6.7 %copy-start.2 = (f32[8,256,512]{2,1,0:T(8,128)S(1)}, f32[8,256,512]{2,1,0:T(8,128)}, u32[]{:S(2)}) copy-start(f32[8,256,512]{2,1,0:T(8,128)} %convert_select_fusion.2) | copy-start | bytes 12582916 | tf_op jit(solution)/shard_map/while
  502.6 2.2 copy-start.3
  507.6 1.0 copy-start.4
  507.6 1.2 copy-start.7
  512.1 4.1 copy-start.9
  512.1 4.1 copy-start.13
  512.1 4.1 copy-start.14
  512.1 44.8 %copy-start.1 = (bf16[128,512]{1,0:T(8,128)(2,1)S(1)}, bf16[128,512]{1,0:T(8,128)(2,1)}, u32[]{:S(2)}) copy-start(bf16[128,512]{1,0:T(8,128)(2,1)} %param.11) | copy-start | bytes 393220
  516.1 1.2 copy-start.6
  516.1 1.2 copy-start.16
  516.1 1.2 copy-start.17
  (9 other events, 7.8 us)
Sparse Core Ops, SparseCore 0:
  9.8 44.5 all-gather.8
  56.9 84.3 all-gather.10
  143.7 83.7 all-gather.12
  229.9 76.7 all-gather.6
  516.3 40.5 reduce-scatter.1
where the time goes:
time: 565 us; the launch traced here: 563 us
  waiting for transfers between devices  302 us (53%)
  local copies, waits for them, and re-layouts  156 us (28%)
  other arithmetic  72.6 us (13%)
  matrix products  17.8 us (3%)
  between operations  14 us (2%)
    gather x16, local copies, waits for them, and re-layouts, fetch(): picked = spec[jnp.clip(indices, 0, block_count - 1)].astype(jnp.float32)  80.8 us
    all_gather x1, waiting for transfers between devices, per_device(): lax.all_gather(own_u, 'seq', axis=0, tiled=True)  78.3 us
    all_gather x1, waiting for transfers between devices, per_device(): lax.all_gather(own_g, 'seq', axis=0, tiled=True)  74.7 us
    all_gather x1, waiting for transfers between devices, per_device(): lax.all_gather(own_h, 'seq', axis=0, tiled=True)  67.1 us
    all_gather x1, waiting for transfers between devices, per_device(): lax.all_gather(out_grad, 'ch', axis=1, tiled=True)  42.8 us
    reduce_scatter x1, waiting for transfers between devices, per_device(): lax.psum_scatter(partial_out.astype(jnp.bfloat16), 'ch', scatter_dimensio...  38.4 us
    add x4, other arithmetic, group_step(): ahead = g_lead + shift_sign * g_next  26.7 us
    unnamed x26, local copies, waits for them, and re-layouts  24.2 us
  transfers between devices with their start and end apart: 5, of which 5 were waited for; matrix products, arithmetic and copies ran while one was open for 7% of the time, Pallas kernels for 0%

commit v1 on v0

--- a/solution.py
+++ b/solution.py
@@ -124,7 +124,9 @@
     table_high, table_low = split_table(forward_t)
     product = (key_act.astype(jnp.float32) * value_act.astype(jnp.float32)).astype(jnp.bfloat16)
     gated_grad = lax.dot_general(
-        lax.all_gather(out_grad, "ch", axis=1, tiled=True),
+        jnp.concatenate(
+            lax.all_to_all(jnp.stack([out_grad] * lax.axis_size("ch")), "ch", 0, 0), axis=1
+        ),
         out_weight,
         (((1,), (1,)), ((), ())),
         preferred_element_type=jnp.float32,

time: 565 us -> 526 us (0.931)
  waiting for transfers between devices: 302 us -> 239 us
  blocking collectives: 0 us -> 23.8 us
    all_gather x1 -> x0, waiting for transfers between devices: 42.8 us -> none  [per_device(): lax.all_gather(out_grad, 'ch', axis=1, tiled=True)]
    all_to_all x0 -> x1, blocking collectives: none -> 23.8 us  [per_device(): lax.all_to_all(jnp.stack([out_grad] * lax.axis_size('ch')), 'ch', 0, 0)]
    all_gather x1, waiting for transfers between devices: 78.3 us -> 58.1 us  [per_device(): lax.all_gather(own_u, 'seq', axis=0, tiled=True)]
    unnamed x26 -> x29, local copies, waits for them, and re-layouts: 24.2 us -> 24 us
  transfers between devices with their start and end apart: 5 -> 4, of which waited for: 5 -> 4; matrix products, arithmetic and copies ran while one was open for 7% -> 6% of each run, Pallas kernels for 0% -> 0%
where the time goes in v1:
time: 526 us; the launch traced here: 524 us
  waiting for transfers between devices  239 us (45%)
  local copies, waits for them, and re-layouts  156 us (30%)
  other arithmetic  72.6 us (14%)
  blocking collectives  23.8 us (5%)
  matrix products  17.5 us (3%)
  between operations  14 us (3%)
    gather x16, local copies, waits for them, and re-layouts, fetch(): picked = spec[jnp.clip(indices, 0, block_count - 1)].astype(jnp.float32)  80.8 us
    all_gather x1, waiting for transfers between devices, per_device(): lax.all_gather(own_g, 'seq', axis=0, tiled=True)  74.9 us
    all_gather x1, waiting for transfers between devices, per_device(): lax.all_gather(own_h, 'seq', axis=0, tiled=True)  67.3 us
    all_gather x1, waiting for transfers between devices, per_device(): lax.all_gather(own_u, 'seq', axis=0, tiled=True)  58.1 us
    reduce_scatter x1, waiting for transfers between devices, per_device(): lax.psum_scatter(partial_out.astype(jnp.bfloat16), 'ch', scatter_dimensio...  38.3 us
    add x4, other arithmetic, group_step(): ahead = g_lead + shift_sign * g_next  26.8 us
    unnamed x29, local copies, waits for them, and re-layouts  24 us
    all_to_all x1, blocking collectives, per_device(): lax.all_to_all(jnp.stack([out_grad] * lax.axis_size('ch')), 'ch', 0, 0)  23.8 us
  transfers between devices with their start and end apart: 4, of which 4 were waited for; matrix products, arithmetic and copies ran while one was open for 6% of the time, Pallas kernels for 0%

profile of v1, /device:TPU:2, one launch (start us, length us, event | category | flops | bytes accessed | tf_op | source)
XLA Modules:
  0.0 523.6 jit_solution(6561821379767867094)
XLA Ops:
  11.1 23.8 %all_to_all.5 = bf16[8,128,512]{1,2,0:T(8,128)(2,1)S(1)} all-to-all(bf16[8,128,512]{1,2,0:T(8,128)(2,1)S(1)} %stack.2), channel_id=1, replica_groups=mesh['seq'=32,'ch'=8] {'ch'}, dimensions={0} | all-to-all | bytes 2097152 | tf_op jit(solution)/shard_map/all_to_all | solution.py:128
  43.1 58.1 %all-gather.8.cloned.1.call-done = bf16[1,8192,512]{1,2,0:T(8,128)(2,1)} async-done(((bf16[1,256,512]{1,2,0:T(8,128)(2,1)}), bf16[1,8192,512]{1,2,0:T(8,128)(2,1)}) %all-gather.8.cloned.1.call-update) | async-done | bytes 8388624 | tf_op jit(solution)/shard_map/all_gather | solution.py:139
  101.2 11.4 %copy.16 = bf16[1,8192,512]{2,1,0:T(8,128)(2,1)} copy(bf16[1,8192,512]{1,2,0:T(8,128)(2,1)} %all-gather.8.cloned.1.call-done) | data formatting | bytes 16777216
  112.5 74.9 %all-gather.10.cloned.1.call-done = bf16[1,8192,512]{1,2,0:T(8,128)(2,1)} async-done(((bf16[1,256,512]{1,2,0:T(8,128)(2,1)}), bf16[1,8192,512]{1,2,0:T(8,128)(2,1)}) %all-gather.10.cloned.1.call-update) | async-done | bytes 8388624 | tf_op jit(solution)/shard_map/all_gather | solution.py:141
  187.5 12.0 %copy.17 = bf16[1,8192,512]{2,1,0:T(8,128)(2,1)} copy(bf16[1,8192,512]{1,2,0:T(8,128)(2,1)} %all-gather.10.cloned.1.call-done) | data formatting | bytes 16777216
  199.5 67.3 %all-gather.6.cloned.1.call-done = bf16[8192,512]{1,0:T(8,128)(2,1)} async-done(((bf16[256,512]{1,0:T(8,128)(2,1)}), bf16[8192,512]{1,0:T(8,128)(2,1)}) %all-gather.6.cloned.1.call-update) | async-done | bytes 8388624 | tf_op jit(solution)/shard_map/all_gather | solution.py:140
  266.8 203.6 %while.21 = (s32[]{:T(128)}, f32[256,512]{1,0:T(8,128)S(1)}, f32[256,512]{1,0:T(8,128)}, f32[256,512]{1,0:T(8,128)}, bf16[32,256,512]{2,1,0:T(8,128)(2,1)}, /*in...) while((s32[]{:T(128)}, f32[256,512]{1,0:T(8,128)S(1)}, ...), condition=%wide.region_4.5_spmd.clone.clone, body=%wide.region_0.4_spmd.clone.clone.sunk | while | flops 38148044 | bytes 155214800 | solution.py:98
  266.8 4.1 gather_fusion
  273.6 5.3 %gather_fusion.1 = bf16[8,256,512]{2,1,0:T(8,128)(2,1)} fusion(bf16[32,256,512]{2,1,0:T(8,128)(2,1)} %get-tuple-element.526, s32[1024]{0:T(1024)S(1)} %pad_clamp_fusion.11), kind=kCustom, calls=%fused_computation.5.clone.clone.1 | custom fusion | bytes 4194336 | tf_op jit(solution)/shard_map/while/body/eval_jaxpr/gather | solution.py:76
  279.0 5.4 %gather_fusion.2 = bf16[8,256,512]{2,1,0:T(8,128)(2,1)} fusion(bf16[32,256,512]{2,1,0:T(8,128)(2,1)} %get-tuple-element.526, s32[1024]{0:T(1024)S(1)} %pad_clamp_fusion.12), kind=kCustom, calls=%fused_computation.4.clone.clone.1 | custom fusion | bytes 4194336 | tf_op jit(solution)/shard_map/while/body/eval_jaxpr/gather | solution.py:76
  284.5 4.1 gather_fusion.3
  288.6 5.4 %gather_fusion.4 = bf16[8,256,512]{2,1,0:T(8,128)(2,1)} fusion(bf16[32,256,512]{2,1,0:T(8,128)(2,1)} %get-tuple-element.522, s32[1024]{0:T(1024)S(1)} %pad_clamp_fusion.14), kind=kCustom, calls=%fused_computation.clone.clone.1 | custom fusion | bytes 4194336 | tf_op jit(solution)/shard_map/while/body/eval_jaxpr/gather | solution.py:76
  293.9 6.7 %multiply_add_fusion.9 = (f32[8,256,512]{2,1,0:T(8,128)}, f32[8,256,512]{2,1,0:T(8,128)S(1)}) fusion(bf16[8,256,512]{2,1,0:T(8,128)(2,1)} %gather_fusion.1, bf16[8,256,512]{2,1,0:T(8,128)(2,1)} %gather_fusion.2, f32[256]{0:T(256)S(1)} %get-tuple-element.523, pred[8]{0:T(512)(128)(4,1)S(1)} %add_compare_fusion.2, pred[8]{0:T(512)(128)(4,1)S(1)} %fusion.88, ...), kind=kLoop, calls=%fused_computation.11.clone.1 | loop fusion | flops 11534336 | bytes 16778264 | tf_op jit(solution)/shard_map/while/body/eval_jaxpr/add | solution.py:93
  302.5 5.5 %gather_fusion.5 = bf16[8,256,512]{2,1,0:T(8,128)(2,1)} fusion(bf16[32,256,512]{2,1,0:T(8,128)(2,1)} %get-tuple-element.525, s32[1024]{0:T(1024)S(1)} %pad_clamp_fusion.13), kind=kCustom, calls=%fused_computation.3.clone.clone.1 | custom fusion | bytes 4194336 | tf_op jit(solution)/shard_map/while/body/eval_jaxpr/gather | solution.py:83
  324.5 5.3 %gather_fusion.1 = bf16[8,256,512]{2,1,0:T(8,128)(2,1)} fusion(bf16[32,256,512]{2,1,0:T(8,128)(2,1)} %get-tuple-element.526, s32[1024]{0:T(1024)S(1)} %pad_clamp_fusion.11), kind=kCustom, calls=%fused_computation.5.clone.clone.1 | custom fusion | bytes 4194336 | tf_op jit(solution)/shard_map/while/body/eval_jaxpr/gather | solution.py:76
  329.9 5.4 %gather_fusion.2 = bf16[8,256,512]{2,1,0:T(8,128)(2,1)} fusion(bf16[32,256,512]{2,1,0:T(8,128)(2,1)} %get-tuple-element.526, s32[1024]{0:T(1024)S(1)} %pad_clamp_fusion.12), kind=kCustom, calls=%fused_computation.4.clone.clone.1 | custom fusion | bytes 4194336 | tf_op jit(solution)/shard_map/while/body/eval_jaxpr/gather | solution.py:76
  335.4 4.1 gather_fusion.3
  339.5 5.4 %gather_fusion.4 = bf16[8,256,512]{2,1,0:T(8,128)(2,1)} fusion(bf16[32,256,512]{2,1,0:T(8,128)(2,1)} %get-tuple-element.522, s32[1024]{0:T(1024)S(1)} %pad_clamp_fusion.14), kind=kCustom, calls=%fused_computation.clone.clone.1 | custom fusion | bytes 4194336 | tf_op jit(solution)/shard_map/while/body/eval_jaxpr/gather | solution.py:76
  344.8 6.7 %multiply_add_fusion.9 = (f32[8,256,512]{2,1,0:T(8,128)}, f32[8,256,512]{2,1,0:T(8,128)S(1)}) fusion(bf16[8,256,512]{2,1,0:T(8,128)(2,1)} %gather_fusion.1, bf16[8,256,512]{2,1,0:T(8,128)(2,1)} %gather_fusion.2, f32[256]{0:T(256)S(1)} %get-tuple-element.523, pred[8]{0:T(512)(128)(4,1)S(1)} %add_compare_fusion.2, pred[8]{0:T(512)(128)(4,1)S(1)} %fusion.88, ...), kind=kLoop, calls=%fused_computation.11.clone.1 | loop fusion | flops 11534336 | bytes 16778264 | tf_op jit(solution)/shard_map/while/body/eval_jaxpr/add | solution.py:93
  353.4 5.5 %gather_fusion.5 = bf16[8,256,512]{2,1,0:T(8,128)(2,1)} fusion(bf16[32,256,512]{2,1,0:T(8,128)(2,1)} %get-tuple-element.525, s32[1024]{0:T(1024)S(1)} %pad_clamp_fusion.13), kind=kCustom, calls=%fused_computation.3.clone.clone.1 | custom fusion | bytes 4194336 | tf_op jit(solution)/shard_map/while/body/eval_jaxpr/gather | solution.py:83
  375.4 5.3 %gather_fusion.1 = bf16[8,256,512]{2,1,0:T(8,128)(2,1)} fusion(bf16[32,256,512]{2,1,0:T(8,128)(2,1)} %get-tuple-element.526, s32[1024]{0:T(1024)S(1)} %pad_clamp_fusion.11), kind=kCustom, calls=%fused_computation.5.clone.clone.1 | custom fusion | bytes 4194336 | tf_op jit(solution)/shard_map/while/body/eval_jaxpr/gather | solution.py:76
  380.8 5.4 %gather_fusion.2 = bf16[8,256,512]{2,1,0:T(8,128)(2,1)} fusion(bf16[32,256,512]{2,1,0:T(8,128)(2,1)} %get-tuple-element.526, s32[1024]{0:T(1024)S(1)} %pad_clamp_fusion.12), kind=kCustom, calls=%fused_computation.4.clone.clone.1 | custom fusion | bytes 4194336 | tf_op jit(solution)/shard_map/while/body/eval_jaxpr/gather | solution.py:76
  390.4 5.4 %gather_fusion.4 = bf16[8,256,512]{2,1,0:T(8,128)(2,1)} fusion(bf16[32,256,512]{2,1,0:T(8,128)(2,1)} %get-tuple-element.522, s32[1024]{0:T(1024)S(1)} %pad_clamp_fusion.14), kind=kCustom, calls=%fused_computation.clone.clone.1 | custom fusion | bytes 4194336 | tf_op jit(solution)/shard_map/while/body/eval_jaxpr/gather | solution.py:76
  395.7 6.7 %multiply_add_fusion.9 = (f32[8,256,512]{2,1,0:T(8,128)}, f32[8,256,512]{2,1,0:T(8,128)S(1)}) fusion(bf16[8,256,512]{2,1,0:T(8,128)(2,1)} %gather_fusion.1, bf16[8,256,512]{2,1,0:T(8,128)(2,1)} %gather_fusion.2, f32[256]{0:T(256)S(1)} %get-tuple-element.523, pred[8]{0:T(512)(128)(4,1)S(1)} %add_compare_fusion.2, pred[8]{0:T(512)(128)(4,1)S(1)} %fusion.88, ...), kind=kLoop, calls=%fused_computation.11.clone.1 | loop fusion | flops 11534336 | bytes 16778264 | tf_op jit(solution)/shard_map/while/body/eval_jaxpr/add | solution.py:93
  404.3 5.5 %gather_fusion.5 = bf16[8,256,512]{2,1,0:T(8,128)(2,1)} fusion(bf16[32,256,512]{2,1,0:T(8,128)(2,1)} %get-tuple-element.525, s32[1024]{0:T(1024)S(1)} %pad_clamp_fusion.13), kind=kCustom, calls=%fused_computation.3.clone.clone.1 | custom fusion | bytes 4194336 | tf_op jit(solution)/shard_map/while/body/eval_jaxpr/gather | solution.py:83
  426.3 5.3 %gather_fusion.1 = bf16[8,256,512]{2,1,0:T(8,128)(2,1)} fusion(bf16[32,256,512]{2,1,0:T(8,128)(2,1)} %get-tuple-element.526, s32[1024]{0:T(1024)S(1)} %pad_clamp_fusion.11), kind=kCustom, calls=%fused_computation.5.clone.clone.1 | custom fusion | bytes 4194336 | tf_op jit(solution)/shard_map/while/body/eval_jaxpr/gather | solution.py:76
  431.7 5.4 %gather_fusion.2 = bf16[8,256,512]{2,1,0:T(8,128)(2,1)} fusion(bf16[32,256,512]{2,1,0:T(8,128)(2,1)} %get-tuple-element.526, s32[1024]{0:T(1024)S(1)} %pad_clamp_fusion.12), kind=kCustom, calls=%fused_computation.4.clone.clone.1 | custom fusion | bytes 4194336 | tf_op jit(solution)/shard_map/while/body/eval_jaxpr/gather | solution.py:76
  441.2 5.4 %gather_fusion.4 = bf16[8,256,512]{2,1,0:T(8,128)(2,1)} fusion(bf16[32,256,512]{2,1,0:T(8,128)(2,1)} %get-tuple-element.522, s32[1024]{0:T(1024)S(1)} %pad_clamp_fusion.14), kind=kCustom, calls=%fused_computation.clone.clone.1 | custom fusion | bytes 4194336 | tf_op jit(solution)/shard_map/while/body/eval_jaxpr/gather | solution.py:76
  446.6 6.7 %multiply_add_fusion.9 = (f32[8,256,512]{2,1,0:T(8,128)}, f32[8,256,512]{2,1,0:T(8,128)S(1)}) fusion(bf16[8,256,512]{2,1,0:T(8,128)(2,1)} %gather_fusion.1, bf16[8,256,512]{2,1,0:T(8,128)(2,1)} %gather_fusion.2, f32[256]{0:T(256)S(1)} %get-tuple-element.523, pred[8]{0:T(512)(128)(4,1)S(1)} %add_compare_fusion.2, pred[8]{0:T(512)(128)(4,1)S(1)} %fusion.88, ...), kind=kLoop, calls=%fused_computation.11.clone.1 | loop fusion | flops 11534336 | bytes 16778264 | tf_op jit(solution)/shard_map/while/body/eval_jaxpr/add | solution.py:93
  455.2 5.5 %gather_fusion.5 = bf16[8,256,512]{2,1,0:T(8,128)(2,1)} fusion(bf16[32,256,512]{2,1,0:T(8,128)(2,1)} %get-tuple-element.525, s32[1024]{0:T(1024)S(1)} %pad_clamp_fusion.13), kind=kCustom, calls=%fused_computation.3.clone.clone.1 | custom fusion | bytes 4194336 | tf_op jit(solution)/shard_map/while/body/eval_jaxpr/gather | solution.py:83
  472.3 4.1 convolution_convert_fusion
  478.7 38.3 %reduce-scatter.2.cloned.1.call-done = bf16[128,512]{1,0:T(8,128)(2,1)} async-done(((bf16[128,4096]{1,0:T(8,128)(2,1)}), bf16[128,512]{1,0:T(8,128)(2,1)}) %reduce-scatter.2.cloned.1.call-update) | async-done | bytes 131088 | tf_op jit(solution)/shard_map/reduce_scatter | solution.py:151
  (216 shorter events, 93.7 us)
Async XLA Ops:
  7.2 33.2 %copy-start = (bf16[128,512]{1,0:T(8,128)(2,1)S(1)}, bf16[128,512]{1,0:T(8,128)(2,1)}, u32[]{:S(2)}) copy-start(bf16[128,512]{1,0:T(8,128)(2,1)} %param.11) | copy-start | bytes 393220
  7.2 3.6 copy-start.18
  7.2 94.0 %all-gather.8.cloned.1.call-start = ((), (), s32[]{:S(2)}) async-start(), calls=%async_computation.4 | async-start | bytes 8650752 | tf_op jit(solution)/shard_map/all_gather | solution.py:139
  10.8 176.7 %all-gather.10.cloned.1.call-start = ((), (), s32[]{:S(2)}) async-start(), calls=%async_computation.5 | async-start | bytes 8650752 | tf_op jit(solution)/shard_map/all_gather | solution.py:141
  34.9 3.8 copy-start.15
  40.3 226.4 %all-gather.6.cloned.1.call-start = ((), (), s32[]{:S(2)}) async-start(), calls=%async_computation.2 | async-start | bytes 8650752 | tf_op jit(solution)/shard_map/all_gather | solution.py:140
  41.6 475.5 %reduce-scatter.2.cloned.1.call-start = ((), (), s32[]{:S(2)}) async-start(), calls=%async_computation.3 | async-start | bytes 1179648 | tf_op jit(solution)/shard_map/reduce_scatter | solution.py:151
  266.8 203.6 %copy-start.11 = (f32[128,512]{1,0:T(8,128)S(1)}, f32[128,512]{1,0:T(8,128)}, u32[]{:S(2)}) copy-start(f32[128,512]{1,0:T(8,128)} %copy-done.10) | copy-start | bytes 786436
  266.8 203.6 %copy-start.12 = (f32[256,128]{1,0:T(8,128)S(1)}, f32[256,128]{1,0:T(8,128)}, u32[]{:S(2)}) copy-start(f32[256,128]{1,0:T(8,128)} %get-tuple-element.413) | copy-start | bytes 393220
  293.9 6.7 %copy-start.2 = (f32[8,256,512]{2,1,0:T(8,128)S(1)}, f32[8,256,512]{2,1,0:T(8,128)}, u32[]{:S(2)}) copy-start(f32[8,256,512]{2,1,0:T(8,128)} %convert_select_fusion.2) | copy-start | bytes 12582916 | tf_op jit(solution)/shard_map/while
  310.2 2.2 copy-start.3
  315.2 1.0 copy-start.4
  315.2 1.2 copy-start.7
  344.8 6.7 %copy-start.2 = (f32[8,256,512]{2,1,0:T(8,128)S(1)}, f32[8,256,512]{2,1,0:T(8,128)}, u32[]{:S(2)}) copy-start(f32[8,256,512]{2,1,0:T(8,128)} %convert_select_fusion.2) | copy-start | bytes 12582916 | tf_op jit(solution)/shard_map/while
  361.1 2.2 copy-start.3
  366.1 1.0 copy-start.4
  366.1 1.2 copy-start.7
  395.7 6.7 %copy-start.2 = (f32[8,256,512]{2,1,0:T(8,128)S(1)}, f32[8,256,512]{2,1,0:T(8,128)}, u32[]{:S(2)}) copy-start(f32[8,256,512]{2,1,0:T(8,128)} %convert_select_fusion.2) | copy-start | bytes 12582916 | tf_op jit(solution)/shard_map/while
  411.9 2.2 copy-start.3
  417.0 1.0 copy-start.4
  417.0 1.2 copy-start.7
  446.6 6.7 %copy-start.2 = (f32[8,256,512]{2,1,0:T(8,128)S(1)}, f32[8,256,512]{2,1,0:T(8,128)}, u32[]{:S(2)}) copy-start(f32[8,256,512]{2,1,0:T(8,128)} %convert_select_fusion.2) | copy-start | bytes 12582916 | tf_op jit(solution)/shard_map/while
  462.8 2.2 copy-start.3
  467.8 1.0 copy-start.4
  467.9 1.2 copy-start.7
  472.3 4.1 copy-start.9
  472.3 4.1 copy-start.13
  472.3 4.1 copy-start.14
  472.3 44.7 %copy-start.1 = (bf16[128,512]{1,0:T(8,128)(2,1)S(1)}, bf16[128,512]{1,0:T(8,128)(2,1)}, u32[]{:S(2)}) copy-start(bf16[128,512]{1,0:T(8,128)(2,1)} %param.11) | copy-start | bytes 393220
  476.4 1.2 copy-start.6
  476.4 1.2 copy-start.16
  476.4 1.2 copy-start.17
  (9 other events, 7.8 us)
Sparse Core Ops, SparseCore 0:
  10.9 90.2 all-gather.7
  103.6 83.7 all-gather.9
  190.0 76.6 all-gather.5
  476.5 40.4 reduce-scatter.1
